TPU v7x, 512 devices: a whole 4x8x8 slice. The times are simulated.
512 devices in a mesh: band: 64 (over x, y, z_hi), pw: 8 (over z_lo, core).
Axes of the slice: x: 4, y: 8, z: 8 (z_hi: 2, z_lo: 4; z = z_hi * 4 + z_lo), core: 2. Of those that a mesh axis runs over, the one named last changes fastest.
Arguments:
- occupied: bfloat16 [2, 64, 4096], P(None, 'pw'), may hold values from -6 to 6
- virtual: bfloat16 [64, 64, 4096], P('band', 'pw'), may hold values from -6 to 6
- screening: bfloat16 [16384, 16384], P('pw', 'band'), may hold values from -0.046875 to 0.046875
- grid_index: int32 [16384], replicated, may hold values from 0 to 262143, as said below
Outputs:
- grad_vir: float32 [64, 64, 4096], P('band', 'pw')
Inputs may be any that keep to these rules, and one draw needn't show every extreme that they name: `grid_index`: all entries are distinct. Write each entry as (kx * 64 + ky) * 64 + kz and take kx, ky, kz as signed frequencies (a value k of 32 or more stands for k - 64): every signed frequency lies within -16 to 16, and some entry has |kx| = |ky| = |kz| = 16. The entries g with g // 2048 = b are grid points whose ky is congruent to b modulo 64 // 8.
All inputs are finite; a program needn't handle non-finite values.
Results may differ from a plain program's by a relative error of at most 0.006.
Values may be sent and summed in bfloat16 or wider, within the bound.
A program may use at most 128 MiB of HBM per device.

v0:
```python
import math
import jax
import jax.numpy as jnp
from jax import lax
from jax.sharding import PartitionSpec as P

GRID = 64
NG = 16384
KMAX = 16
NK = 2 * KMAX + 1
PW = 8
BAND = 64
NJ = 5
PRECISE = lax.Precision.HIGHEST
F32 = jnp.float32
BF16 = jnp.bfloat16


def phases(left, right):
    angles = (left[:, None] * right[None, :] % GRID).astype(F32) * (2.0 * math.pi / GRID)
    return (jnp.cos(angles), jnp.sin(angles))


def dot(spec, a, b):
    return jnp.einsum(spec, a, b, precision=PRECISE, preferred_element_type=F32)


def body(occupied, virtual, screening, grid_index):
    pairs, planes = (occupied.shape[0], occupied.shape[1])
    slab = lax.axis_index("pw")
    cells = jnp.arange(GRID, dtype=jnp.int32)
    freqs = jnp.arange(NK, dtype=jnp.int32) - KMAX
    row_freqs = (
        jnp.arange(PW, dtype=jnp.int32)[:, None] - KMAX + PW * jnp.arange(NJ, dtype=jnp.int32)[None]
    )
    cos_k, sin_k = phases(cells, freqs)
    cos_y, sin_y = phases(cells, row_freqs.reshape(-1))
    block = NG // PW
    own = lax.dynamic_slice_in_dim(grid_index, slab * block, block)

    def signed(k):
        return jnp.where(k >= GRID // 2, k - GRID, k)

    at_x = signed(own // (GRID * GRID)) + KMAX
    at_j = (signed(own // GRID % GRID) + KMAX - slab) // PW
    at_z = signed(own % GRID) + KMAX
    at_jz = at_j * NK + at_z
    pick_x = (jnp.arange(NK, dtype=jnp.int32)[:, None] == at_x[None]).astype(BF16)
    pick_jz = jnp.arange(NJ * NK, dtype=jnp.int32)[:, None] == at_jz[None]
    density = occupied.astype(F32) * virtual.astype(F32)
    density = density.reshape(pairs, planes, GRID, GRID)
    forward_z = jnp.concatenate([cos_k, -sin_k], axis=1)
    field = dot("pxyz,zc->pxyc", density, forward_z)
    both_y = jnp.concatenate([cos_y, sin_y], axis=1)
    mixed = dot("pxyc,yk->pxkc", field, both_y).reshape(pairs, planes, 2, PW, NJ, 2, NK)
    real = mixed[:, :, 0, :, :, 0] + mixed[:, :, 1, :, :, 1]
    imag = mixed[:, :, 0, :, :, 1] - mixed[:, :, 1, :, :, 0]
    field = jnp.stack([real, imag], axis=0).astype(BF16)
    field = field.transpose(3, 2, 1, 0, 4, 5).reshape(PW, planes, pairs * 2 * NJ * NK)
    pencil = lax.all_to_all(field, "pw", 0, 0, tiled=True).reshape(GRID, -1)
    cos_sin = jnp.concatenate([cos_k, sin_k], axis=1)
    mixed = dot("xm,xk->mk", pencil.astype(F32), cos_sin).reshape(pairs, 2, NJ * NK, 2, NK)
    real = mixed[:, 0, :, 0] + mixed[:, 1, :, 1]
    imag = mixed[:, 1, :, 0] - mixed[:, 0, :, 1]
    box = (jnp.stack([real, imag], axis=1) * (1.0 / math.sqrt(GRID**3))).astype(BF16)
    columns = jnp.einsum("prmk,kg->prmg", box, pick_x, preferred_element_type=F32)
    spectra = jnp.sum(jnp.where(pick_jz[None, None], columns, 0.0), axis=2).astype(BF16)
    rows = pairs * 2
    everyone = lax.all_gather(spectra.reshape(rows, block), "band", axis=0, tiled=True)
    partial = jnp.dot(everyone, screening, preferred_element_type=F32).astype(BF16)
    width = screening.shape[1]
    partial = lax.all_to_all(partial.reshape(PW, PW * rows, width), "pw", 0, 0, tiled=True)
    summed = jnp.sum(partial.astype(F32), axis=0).astype(BF16).reshape(PW, rows, width)
    turn = []
    for c1 in range(PW):
        for c0 in range(PW):
            for p in range(PW):
                turn.append(((c1 * PW + c0) * PW + p, (p * PW + c0) * PW + c1))
    summed = lax.ppermute(summed, ("band", "pw"), turn)
    groups = [[PW * k + t for t in range(PW)] for k in range(BAND // PW)]
    home = lax.all_to_all(summed, "band", 0, 0, axis_index_groups=groups, tiled=True)
    screened = home.transpose(1, 0, 2).reshape(rows, 1, block)
    spread = jnp.where(pick_jz[None], screened, jnp.zeros((), BF16)).reshape(rows * NJ * NK, block)
    box = jnp.einsum("mg,kg->mk", spread, pick_x, preferred_element_type=F32)
    mixed = dot("xk,mk->xm", jnp.concatenate([cos_k, sin_k], axis=0), box)
    mixed = mixed.reshape(2, GRID, pairs, 2, NJ * NK)
    real = mixed[0, :, :, 0] - mixed[1, :, :, 1]
    imag = mixed[0, :, :, 1] + mixed[1, :, :, 0]
    pencil = jnp.stack([real, imag], axis=2).astype(BF16).reshape(PW, planes, -1)
    field = lax.all_to_all(pencil, "pw", 0, 0, tiled=True)
    field = field.reshape(PW, planes, pairs, 2, NJ, NK).astype(F32)
    field = field.transpose(2, 1, 0, 4, 3, 5).reshape(pairs, planes, PW * NJ, 2 * NK)
    mixed = dot("pxkc,yk->pxyc", field, jnp.concatenate([cos_y, sin_y], axis=0))
    mixed = mixed.reshape(pairs, planes, 2, GRID, 2 * NK)
    mixed = jnp.concatenate([mixed[:, :, 0], mixed[:, :, 1]], axis=-1)
    cz, sz = (jnp.transpose(cos_k), jnp.transpose(sin_k))
    back = jnp.concatenate([cz, -sz, -sz, -cz], axis=0) * (1.0 / math.sqrt(NG))
    potential = dot("pxyc,cz->pxyz", mixed, back)
    weighted = potential.reshape(pairs, planes, GRID * GRID) * occupied.astype(F32)
    return jnp.sum(weighted, axis=0)[None]


def solution(mesh):
    return jax.shard_map(
        body,
        mesh=mesh,
        in_specs=(P(None, "pw", None), P("band", "pw", None), P("pw", "band"), P()),
        out_specs=P("band", "pw", None),
        check_vma=False,
    )
```

profile of v0, /device:TPU:1, one launch (start us, length us, event | category | flops | bytes accessed | tf_op | source)
XLA Modules:
  0.0 234.0 jit_solution(1686862326288065486)
XLA Ops:
  6.5 0.0 copy-start
  6.5 0.2 fusion.68
  6.7 0.9 bitcast_convert_fusion
  7.7 0.9 convert_multiply_fusion.1
  8.6 0.2 reshape.230
  8.8 0.1 broadcast_add_fusion
  8.9 0.1 add.166
  9.0 0.2 fusion.71
  9.2 0.6 fusion.37
  9.7 1.1 convolution_bitcast_fusion.1
  10.9 0.3 copy.91
  11.1 0.8 reshape.231
  11.9 1.0 fusion.90
  12.9 0.1 fusion.10
  13.0 0.1 maximum_bitcast_fusion
  13.1 0.1 copy.96
  13.2 1.2 reshape.232
  14.4 10.1 %all-to-all-start = ((bf16[8,8,660]{2,1,0:T(8,128)(2,1)}), bf16[8,8,660]{2,1,0:T(8,128)(2,1)S(1)}, u32[]{:S(2)}, u32[]{:S(2)}) async-start(bf16[8,8,660]{2,1,0:T(8,128)(2,1)} %reshape.232), calls=%async_computation | async-start | bytes 196608 | tf_op jit(solution)/shard_map/all_to_all | solution.py:60
  24.5 0.0 all-gather.3.cloned.1.call-start
  24.5 0.7 fusion.80
  25.2 0.7 fusion.75
  25.9 0.2 iota_compare_fusion
  26.2 3.7 %all-to-all-done = bf16[8,8,660]{2,1,0:T(8,128)(2,1)S(1)} async-done(((bf16[8,8,660]{2,1,0:T(8,128)(2,1)}), bf16[8,8,660]{2,1,0:T(8,128)(2,1)S(1)}, u32[]{:S(2)}, u32[]{:S(2)}) %all-to-all-start) | async-done | bytes 84512 | tf_op jit(solution)/shard_map/all_to_all | solution.py:60
  29.9 0.1 dot_general.38
  30.0 0.3 fusion.17
  30.4 1.0 select_reduce_fusion
  31.4 0.6 reshape.242
  32.0 0.0 all-gather.3.cloned.1.call-update
  32.0 127.1 %all-gather.3.cloned.1.call-done = bf16[64,4,2048]{2,1,0:T(4,128)(2,1)} async-done(((bf16[1,4,2048]{2,1,0:T(4,128)(2,1)}), bf16[64,4,2048]{2,1,0:T(4,128)(2,1)}) %all-gather.3.cloned.1.call-update) | async-done | bytes 1048592 | tf_op jit(solution)/shard_map/all_gather | solution.py:69
  159.1 1.3 reshape.243
  160.5 0.0 copy-done
  160.5 0.4 convolution_convert_fusion
  160.9 13.9 %all_to_all.20 = bf16[8,32,256]{2,1,0:T(8,128)(2,1)S(1)} all-to-all(bf16[8,32,256]{2,1,0:T(8,128)(2,1)S(1)} %bitcast.87), channel_id=1, replica_groups=mesh['band'=64,'pw'=8] {'pw'}, dimensions={0} | all-to-all | bytes 262144 | tf_op jit(solution)/shard_map/all_to_all | solution.py:72
  174.9 4.9 %collective-permute-start = (bf16[8,4,256]{2,1,0:T(4,128)(2,1)S(1)}, bf16[8,4,256]{2,1,0:T(4,128)(2,1)S(1)}, u32[]{:S(2)}, u32[]{:S(2)}) collective-permute-start(bf16[8,4,256]{2,1,0:T(4,128)(2,1)S(1)} %reshape.235), channel_id=1, source_target_pairs={{0,0},{1,64},{2,128},{3,192},{4,256},{5,320},{6,384},{7,448},{8,8}... | collective-permute-start | bytes 49160 | tf_op jit(solution)/shard_map/ppermute | solution.py:79
  179.8 4.1 %collective-permute-done = bf16[8,4,256]{2,1,0:T(4,128)(2,1)S(1)} collective-permute-done((bf16[8,4,256]{2,1,0:T(4,128)(2,1)S(1)}, bf16[8,4,256]{2,1,0:T(4,128)(2,1)S(1)}, u32[]{:S(2)}, u32[]{:S(2)}) %collective-permute-start) | collective-permute-done | bytes 16416 | tf_op jit(solution)/shard_map/ppermute | solution.py:79
  183.8 12.4 %all_to_all.21 = bf16[8,4,256]{2,1,0:T(4,128)(2,1)S(1)} all-to-all(bf16[8,4,256]{2,1,0:T(4,128)(2,1)S(1)} %collective-permute-done), channel_id=1, replica_groups={{0,8,16,24,32,40,48,56},{64,72,80,88,96,104,112,120},{128,136,144,152,1..., dimensions={0} | all-to-all | bytes 32768 | tf_op jit(solution)/shard_map/all_to_all | solution.py:81
  196.3 2.0 broadcast_select_fusion
  198.2 4.1 %select_n.97 = bf16[660,2048]{1,0:T(8,128)(2,1)} reshape(bf16[4,165,2048]{2,1,0:T(8,128)(2,1)} %broadcast_select_fusion) | data formatting | bytes 5406720 | tf_op jit(solution)/shard_map/jit(_where)/select_n | solution.py:83
  202.3 2.7 %fusion.6 = f32[660,33]{0,1:T(8,128)S(1)} fusion(bf16[660,2048]{1,0:T(8,128)(2,1)} %select_n.97, s32[2048]{0:T(1024)S(1)} %get-tuple-element.5), kind=kOutput, calls=%fused_computation.18 | convolution fusion | flops 89278464 | bytes 2798672 | tf_op jit(solution)/shard_map/mg,kg->mk/dot_general | solution.py:84
  205.0 0.6 fusion.56
  205.6 0.8 reshape.236
  206.4 0.4 fusion.92
  206.9 0.1 copy.106
  207.0 0.8 convert_element_type.68
  207.8 7.9 %all-to-all-start.3 = ((bf16[8,8,660]{2,1,0:T(8,128)(2,1)}), bf16[8,8,660]{2,1,0:T(8,128)(2,1)S(1)}, u32[]{:S(2)}, u32[]{:S(2)}) async-start(bf16[8,8,660]{2,1,0:T(8,128)(2,1)} %convert_element_type.68), calls=%async_computation.3 | async-start | bytes 196608 | tf_op jit(solution)/shard_map/all_to_all | solution.py:90
  215.7 0.2 fusion.66
  215.9 5.2 %all-to-all-done.3 = bf16[8,8,660]{2,1,0:T(8,128)(2,1)S(1)} async-done(((bf16[8,8,660]{2,1,0:T(8,128)(2,1)}), bf16[8,8,660]{2,1,0:T(8,128)(2,1)S(1)}, u32[]{:S(2)}, u32[]{:S(2)}) %all-to-all-start.3) | async-done | bytes 84512 | tf_op jit(solution)/shard_map/all_to_all | solution.py:90
  221.1 0.9 reshape.237
  222.0 0.3 copy.107
  222.3 0.2 reshape.238
  222.5 0.5 convolution_bitcast_fusion
  223.0 0.6 reshape.253
  223.6 0.8 fusion.91
  224.4 0.0 copy-start.1
  224.4 0.4 copy.135
  224.8 0.4 copy.136
  225.2 1.1 fusion
  226.3 0.2 reshape.240
  226.5 0.0 copy-done.1
  226.5 0.7 fusion.9
  (12 shorter events, 0.1 us)
Async XLA Ops:
  6.5 153.9 %copy-start = (bf16[2048,256]{1,0:T(8,128)(2,1)S(1)}, bf16[2048,256]{1,0:T(8,128)(2,1)}, u32[]{:S(2)}) copy-start(bf16[2048,256]{1,0:T(8,128)(2,1)} %param.6) | copy-start | bytes 3145732
  14.4 15.5 %all-to-all-start = ((bf16[8,8,660]{2,1,0:T(8,128)(2,1)}), bf16[8,8,660]{2,1,0:T(8,128)(2,1)S(1)}, u32[]{:S(2)}, u32[]{:S(2)}) async-start(bf16[8,8,660]{2,1,0:T(8,128)(2,1)} %reshape.232), calls=%async_computation | async-start | bytes 196608 | tf_op jit(solution)/shard_map/all_to_all | solution.py:60
  24.5 134.6 %all-gather.3.cloned.1.call-start = ((), (), s32[]{:S(2)}) async-start(), calls=%async_computation.4 | async-start | bytes 1064960 | tf_op jit(solution)/shard_map/all_gather | solution.py:69
  174.9 9.0 %collective-permute-start = (bf16[8,4,256]{2,1,0:T(4,128)(2,1)S(1)}, bf16[8,4,256]{2,1,0:T(4,128)(2,1)S(1)}, u32[]{:S(2)}, u32[]{:S(2)}) collective-permute-start(bf16[8,4,256]{2,1,0:T(4,128)(2,1)S(1)} %reshape.235), channel_id=1, source_target_pairs={{0,0},{1,64},{2,128},{3,192},{4,256},{5,320},{6,384},{7,448},{8,8}... | collective-permute-start | bytes 49160 | tf_op jit(solution)/shard_map/ppermute | solution.py:79
  207.8 13.3 %all-to-all-start.3 = ((bf16[8,8,660]{2,1,0:T(8,128)(2,1)}), bf16[8,8,660]{2,1,0:T(8,128)(2,1)S(1)}, u32[]{:S(2)}, u32[]{:S(2)}) async-start(bf16[8,8,660]{2,1,0:T(8,128)(2,1)} %convert_element_type.68), calls=%async_computation.3 | async-start | bytes 196608 | tf_op jit(solution)/shard_map/all_to_all | solution.py:90
  224.4 2.1 copy-start.1
Sparse Core Ops, SparseCore 0:
  32.2 126.9 all-gather.2
where the time goes:
time: 235 us; the launch traced here: 234 us
  waiting for transfers between devices  140 us (60%)
  blocking collectives  26.3 us (11%)
  starting transfers between devices  22.9 us (10%)
  local copies, waits for them, and re-layouts  15.7 us (7%)
  between operations  13.7 us (6%)
  matrix products  8.27 us (4%)
  other arithmetic  7 us (3%)
    all_gather x1, waiting for transfers between devices, body(): lax.all_gather(spectra.reshape(rows, block), 'band', axis=0, tiled=True)  127 us
    all_to_all x1, blocking collectives, body(): lax.all_to_all(partial.reshape(PW, PW * rows, width), 'pw', 0, 0, tiled=T...  13.9 us
    all_to_all x1, blocking collectives, body(): lax.all_to_all(summed, 'band', 0, 0, axis_index_groups=groups, tiled=True)  12.4 us
    all_to_all x1, starting transfers between devices, body(): pencil = lax.all_to_all(field, 'pw', 0, 0, tiled=True).reshape(GRID, -1)  10.1 us
    all_to_all x1, starting transfers between devices, body(): field = lax.all_to_all(pencil, 'pw', 0, 0, tiled=True)  7.91 us
    all_to_all x1, waiting for transfers between devices, body(): field = lax.all_to_all(pencil, 'pw', 0, 0, tiled=True)  5.21 us
    ppermute x1, starting transfers between devices, body(): summed = lax.ppermute(summed, ('band', 'pw'), turn)  4.9 us
  transfers between devices with their start and end apart: 4, of which 4 were waited for; matrix products, arithmetic and copies ran while one was open for 1% of the time, Pallas kernels for 0%

commit v1 on v0

--- a/solution.py
+++ b/solution.py
@@ -66,7 +66,12 @@
     columns = jnp.einsum("prmk,kg->prmg", box, pick_x, preferred_element_type=F32)
     spectra = jnp.sum(jnp.where(pick_jz[None, None], columns, 0.0), axis=2).astype(BF16)
     rows = pairs * 2
-    everyone = lax.all_gather(spectra.reshape(rows, block), "band", axis=0, tiled=True)
+    everyone = jnp.concatenate(
+        lax.all_to_all(
+            jnp.stack([spectra.reshape(rows, block)] * lax.axis_size("band")), "band", 0, 0
+        ),
+        axis=0,
+    )
     partial = jnp.dot(everyone, screening, preferred_element_type=F32).astype(BF16)
     width = screening.shape[1]
     partial = lax.all_to_all(partial.reshape(PW, PW * rows, width), "pw", 0, 0, tiled=True)

time: 235 us -> 136 us (0.58)
  waiting for transfers between devices: 140 us -> 12.4 us
  blocking collectives: 26.3 us -> 69.2 us
  between operations: 13.7 us -> 0.4 us
    all_gather x1 -> x0, waiting for transfers between devices: 127 us -> none  [body(): lax.all_gather(spectra.reshape(rows, block), 'band', axis=0, tiled=True)]
    all_to_all x0 -> x1, blocking collectives: none -> 45.2 us  [body(): lax.all_to_all(jnp.stack([spectra.reshape(rows, block)] * lax.axis_size('...]
    all_to_all x1, blocking collectives: 13.9 us -> 11.2 us  [body(): lax.all_to_all(partial.reshape(PW, PW * rows, width), 'pw', 0, 0, tiled=T...]
  transfers between devices with their start and end apart: 4 -> 3, of which waited for: 4 -> 3; matrix products, arithmetic and copies ran while one was open for 1% -> 1% of each run, Pallas kernels for 0% -> 0%
where the time goes in v1:
time: 136 us; the launch traced here: 135 us
  blocking collectives  69.2 us (51%)
  starting transfers between devices  23.3 us (17%)
  local copies, waits for them, and re-layouts  14.6 us (11%)
  waiting for transfers between devices  12.4 us (9%)
  matrix products  8.26 us (6%)
  other arithmetic  7.01 us (5%)
    all_to_all x1, blocking collectives, body(): lax.all_to_all(jnp.stack([spectra.reshape(rows, block)] * lax.axis_size('...  45.2 us
    all_to_all x1, blocking collectives, body(): lax.all_to_all(summed, 'band', 0, 0, axis_index_groups=groups, tiled=True)  12.8 us
    all_to_all x1, blocking collectives, body(): lax.all_to_all(partial.reshape(PW, PW * rows, width), 'pw', 0, 0, tiled=T...  11.2 us
    all_to_all x1, starting transfers between devices, body(): pencil = lax.all_to_all(field, 'pw', 0, 0, tiled=True).reshape(GRID, -1)  10.1 us
    all_to_all x1, starting transfers between devices, body(): field = lax.all_to_all(pencil, 'pw', 0, 0, tiled=True)  7.74 us
    ppermute x1, starting transfers between devices, body(): summed = lax.ppermute(summed, ('band', 'pw'), turn)  5.47 us
    all_to_all x1, waiting for transfers between devices, body(): field = lax.all_to_all(pencil, 'pw', 0, 0, tiled=True)  5.21 us
    dot_general x6, matrix products, dot(): return jnp.einsum(spec, a, b, precision=PRECISE, preferred_element_type=F32)  4.12 us
  transfers between devices with their start and end apart: 3, of which 3 were waited for; matrix products, arithmetic and copies ran while one was open for 1% of the time, Pallas kernels for 0%

profile of v1, /device:TPU:1, one launch (start us, length us, event | category | flops | bytes accessed | tf_op | source)
XLA Modules:
  0.0 135.2 jit_solution(6816391122266474367)
XLA Ops:
  0.0 0.0 copy-start
  0.0 0.2 fusion.68
  0.2 0.9 bitcast_convert_fusion
  1.1 0.9 convert_multiply_fusion.1
  2.1 0.2 reshape.234
  2.3 0.1 broadcast_add_fusion
  2.4 0.1 add.166
  2.5 0.2 fusion.71
  2.6 0.0 copy-start.2
  2.6 0.6 fusion.37
  3.2 1.1 convolution_bitcast_fusion.1
  4.3 0.0 copy-done.2
  4.4 0.3 copy.91
  4.6 0.8 reshape.235
  5.4 1.0 fusion.90
  6.4 0.1 fusion.10
  6.5 0.1 maximum_bitcast_fusion
  6.6 0.1 copy.96
  6.7 1.2 reshape.236
  7.9 10.1 %all-to-all-start = ((bf16[8,8,660]{2,1,0:T(8,128)(2,1)}), bf16[8,8,660]{2,1,0:T(8,128)(2,1)S(1)}, u32[]{:S(2)}, u32[]{:S(2)}) async-start(bf16[8,8,660]{2,1,0:T(8,128)(2,1)} %reshape.236), calls=%async_computation | async-start | bytes 196608 | tf_op jit(solution)/shard_map/all_to_all | solution.py:60
  18.0 0.7 fusion.80
  18.7 0.0 copy-start.4
  18.7 0.7 fusion.75
  19.4 0.2 iota_compare_fusion
  19.7 3.7 %all-to-all-done = bf16[8,8,660]{2,1,0:T(8,128)(2,1)S(1)} async-done(((bf16[8,8,660]{2,1,0:T(8,128)(2,1)}), bf16[8,8,660]{2,1,0:T(8,128)(2,1)S(1)}, u32[]{:S(2)}, u32[]{:S(2)}) %all-to-all-start) | async-done | bytes 84512 | tf_op jit(solution)/shard_map/all_to_all | solution.py:60
  23.4 0.1 dot_general.38
  23.5 0.3 fusion.17
  23.8 1.0 select_reduce_fusion
  24.9 0.0 copy-done.4
  24.9 0.5 stack.22
  25.4 45.2 %all_to_all.25 = bf16[64,4,2048]{2,1,0:T(4,128)(2,1)S(1)} all-to-all(bf16[64,4,2048]{2,1,0:T(4,128)(2,1)S(1)} %stack.22), channel_id=1, replica_groups=mesh['band'=64,'pw'=8] {'band'}, dimensions={0} | all-to-all | bytes 2097152 | tf_op jit(solution)/shard_map/all_to_all | solution.py:70
  70.6 0.3 reshape.238
  70.9 0.0 copy-done
  70.9 0.4 convolution_convert_fusion
  71.3 11.2 %all_to_all.26 = bf16[8,32,256]{2,1,0:T(8,128)(2,1)S(1)} all-to-all(bf16[8,32,256]{2,1,0:T(8,128)(2,1)S(1)} %bitcast.87), channel_id=1, replica_groups=mesh['band'=64,'pw'=8] {'pw'}, dimensions={0} | all-to-all | bytes 262144 | tf_op jit(solution)/shard_map/all_to_all | solution.py:77
  82.6 5.5 %collective-permute-start = (bf16[8,4,256]{2,1,0:T(4,128)(2,1)S(1)}, bf16[8,4,256]{2,1,0:T(4,128)(2,1)S(1)}, u32[]{:S(2)}, u32[]{:S(2)}) collective-permute-start(bf16[8,4,256]{2,1,0:T(4,128)(2,1)S(1)} %reshape.240), channel_id=1, source_target_pairs={{0,0},{1,64},{2,128},{3,192},{4,256},{5,320},{6,384},{7,448},{8,8}... | collective-permute-start | bytes 49160 | tf_op jit(solution)/shard_map/ppermute | solution.py:84
  88.0 3.5 %collective-permute-done = bf16[8,4,256]{2,1,0:T(4,128)(2,1)S(1)} collective-permute-done((bf16[8,4,256]{2,1,0:T(4,128)(2,1)S(1)}, bf16[8,4,256]{2,1,0:T(4,128)(2,1)S(1)}, u32[]{:S(2)}, u32[]{:S(2)}) %collective-permute-start) | collective-permute-done | bytes 16416 | tf_op jit(solution)/shard_map/ppermute | solution.py:84
  91.5 12.8 %all_to_all.27 = bf16[8,4,256]{2,1,0:T(4,128)(2,1)S(1)} all-to-all(bf16[8,4,256]{2,1,0:T(4,128)(2,1)S(1)} %collective-permute-done), channel_id=1, replica_groups={{0,8,16,24,32,40,48,56},{64,72,80,88,96,104,112,120},{128,136,144,152,1..., dimensions={0} | all-to-all | bytes 32768 | tf_op jit(solution)/shard_map/all_to_all | solution.py:86
  104.4 2.0 %broadcast_select_fusion = bf16[4,165,2048]{2,1,0:T(8,128)(2,1)} fusion(pred[165,2048]{1,0:T(8,128)(4,1)S(1)} %iota_compare_fusion, bf16[4,2048]{1,0:T(4,128)(2,1)S(1)} %bitcast.90), kind=kLoop, calls=%fused_computation.1 | loop fusion | flops 1351680 | bytes 3057664 | tf_op jit(solution)/shard_map/jit(_where)/select_n | solution.py:88
  106.3 4.1 %select_n.97 = bf16[660,2048]{1,0:T(8,128)(2,1)} reshape(bf16[4,165,2048]{2,1,0:T(8,128)(2,1)} %broadcast_select_fusion) | data formatting | bytes 5406720 | tf_op jit(solution)/shard_map/jit(_where)/select_n | solution.py:88
  110.4 0.0 copy-done.5
  110.4 2.7 %fusion.6 = f32[660,33]{0,1:T(8,128)S(1)} fusion(bf16[660,2048]{1,0:T(8,128)(2,1)} %select_n.97, s32[2048]{0:T(1024)S(1)} %copy-done.5), kind=kOutput, calls=%fused_computation.18 | convolution fusion | flops 89278464 | bytes 2798672 | tf_op jit(solution)/shard_map/mg,kg->mk/dot_general | solution.py:89
  113.1 0.6 fusion.56
  113.7 0.0 copy-start.3
  113.7 0.8 reshape.241
  114.6 0.4 fusion.92
  115.1 0.1 copy.106
  115.2 0.8 convert_element_type.69
  116.0 7.7 %all-to-all-start.4 = ((bf16[8,8,660]{2,1,0:T(8,128)(2,1)}), bf16[8,8,660]{2,1,0:T(8,128)(2,1)S(1)}, u32[]{:S(2)}, u32[]{:S(2)}) async-start(bf16[8,8,660]{2,1,0:T(8,128)(2,1)} %convert_element_type.69), calls=%async_computation.4 | async-start | bytes 196608 | tf_op jit(solution)/shard_map/all_to_all | solution.py:95
  123.7 0.2 fusion.66
  123.9 5.2 %all-to-all-done.4 = bf16[8,8,660]{2,1,0:T(8,128)(2,1)S(1)} async-done(((bf16[8,8,660]{2,1,0:T(8,128)(2,1)}), bf16[8,8,660]{2,1,0:T(8,128)(2,1)S(1)}, u32[]{:S(2)}, u32[]{:S(2)}) %all-to-all-start.4) | async-done | bytes 84512 | tf_op jit(solution)/shard_map/all_to_all | solution.py:95
  129.1 0.9 reshape.242
  130.0 0.3 copy.107
  130.3 0.2 reshape.243
  130.5 0.0 copy-done.3
  130.5 0.5 convolution_bitcast_fusion
  131.0 0.6 reshape.255
  131.6 0.8 fusion.91
  132.5 0.0 copy-start.1
  132.5 0.4 copy.135
  132.9 0.4 copy.136
  133.3 1.1 fusion
  134.3 0.2 reshape.245
  134.5 0.7 fusion.9
  (15 shorter events, 0.2 us)
Async XLA Ops:
  0.0 70.9 %copy-start = (bf16[2048,256]{1,0:T(8,128)(2,1)S(1)}, bf16[2048,256]{1,0:T(8,128)(2,1)}, u32[]{:S(2)}) copy-start(bf16[2048,256]{1,0:T(8,128)(2,1)} %param.6) | copy-start | bytes 3145732
  2.6 1.7 %copy-start.2 = (f32[64,40]{0,1:T(8,128)}, f32[64,40]{0,1:T(8,128)S(1)}, u32[]{:S(2)}) copy-start(f32[64,40]{0,1:T(8,128)S(1)} %get-tuple-element.24) | copy-start | bytes 30724
  7.9 15.5 %all-to-all-start = ((bf16[8,8,660]{2,1,0:T(8,128)(2,1)}), bf16[8,8,660]{2,1,0:T(8,128)(2,1)S(1)}, u32[]{:S(2)}, u32[]{:S(2)}) async-start(bf16[8,8,660]{2,1,0:T(8,128)(2,1)} %reshape.236), calls=%async_computation | async-start | bytes 196608 | tf_op jit(solution)/shard_map/all_to_all | solution.py:60
  18.7 6.2 %copy-start.4 = (s32[2048]{0:T(1024)}, s32[2048]{0:T(1024)S(1)}, u32[]{:S(2)}) copy-start(s32[2048]{0:T(1024)S(1)} %get-tuple-element.5) | copy-start | bytes 24580
  82.6 9.0 %collective-permute-start = (bf16[8,4,256]{2,1,0:T(4,128)(2,1)S(1)}, bf16[8,4,256]{2,1,0:T(4,128)(2,1)S(1)}, u32[]{:S(2)}, u32[]{:S(2)}) collective-permute-start(bf16[8,4,256]{2,1,0:T(4,128)(2,1)S(1)} %reshape.240), channel_id=1, source_target_pairs={{0,0},{1,64},{2,128},{3,192},{4,256},{5,320},{6,384},{7,448},{8,8}... | collective-permute-start | bytes 49160 | tf_op jit(solution)/shard_map/ppermute | solution.py:84
  106.3 4.1 %copy-start.5 = (s32[2048]{0:T(1024)S(1)}, s32[2048]{0:T(1024)}, u32[]{:S(2)}) copy-start(s32[2048]{0:T(1024)} %copy-done.4) | copy-start | bytes 24580
  113.7 16.7 %copy-start.3 = (f32[64,40]{0,1:T(8,128)S(1)}, f32[64,40]{0,1:T(8,128)}, u32[]{:S(2)}) copy-start(f32[64,40]{0,1:T(8,128)} %copy-done.2) | copy-start | bytes 30724
  116.0 13.1 %all-to-all-start.4 = ((bf16[8,8,660]{2,1,0:T(8,128)(2,1)}), bf16[8,8,660]{2,1,0:T(8,128)(2,1)S(1)}, u32[]{:S(2)}, u32[]{:S(2)}) async-start(bf16[8,8,660]{2,1,0:T(8,128)(2,1)} %convert_element_type.69), calls=%async_computation.4 | async-start | bytes 196608 | tf_op jit(solution)/shard_map/all_to_all | solution.py:95
  132.5 2.1 %copy-start.1 = (bf16[2,8,4096]{2,1,0:T(8,128)(2,1)S(1)}, bf16[2,8,4096]{2,1,0:T(8,128)(2,1)}, u32[]{:S(2)}) copy-start(bf16[2,8,4096]{2,1,0:T(8,128)(2,1)} %param.4) | copy-start | bytes 393220
